TPU v7x, 512 devices: a whole 4x8x8 slice. The times are simulated.
512 devices in a mesh: row: 64 (over y, z), col: 8 (over x, core).
Axes of the slice: x: 4, y: 8, z: 8, core: 2. Of those that a mesh axis runs over, the one named last changes fastest.
Arguments:
- object_field: float32 [2, 16384, 2048], P(None, 'row', 'col'), may hold values from -6 to 6
- probe_field: float32 [2, 256, 256], replicated, may hold values from -6 to 6
- amplitudes: float32 [128, 2048, 256], P('row', 'col'), may hold values from 0 to 4
- offsets: int32 [64, 8, 2, 2], P('row', 'col'), may hold values from 0 to 128, as said below
- counts: int32 [64, 8], P('row', 'col'), may hold values from 1 to 2
Outputs:
- object_out: float32 [2, 16384, 2048], P(None, 'row', 'col')
- probe_out: float32 [2, 256, 256], replicated
Inputs may be any that keep to these rules, and one draw needn't show every extreme that they name: `offsets`: slots from counts[r, c] on are padding and hold no window.
All inputs are finite; a program needn't handle non-finite values.
Results may differ from a plain program's by a relative error of at most 0.0003.
Values sent between devices are 32-bit elements; how exact they have to be, the bound alone decides.
No kernel may reach another device: no remote copies, remote signals or barrier semaphores. Data moves between devices by JAX's collectives and lax.ppermute only.
A program may use at most 64 MiB of HBM per device.

v0:
```python
import math
import jax
import jax.numpy as jnp
from jax import lax
from jax.sharding import PartitionSpec as P

HALO = 128
OUTER = 2
smooth_floor = 0.5
object_step = 0.5
tiny_value = 1e-06


def shifted(value, axis, by):
    length = lax.axis_size(axis)
    pairs = [(i, i + by) for i in range(length) if 0 <= i + by < length]
    return lax.ppermute(value, axis, pairs)


def make_tables(length):
    indices = jnp.arange(length, dtype=jnp.int32)
    product = indices[:, None] * indices[None, :] % length
    angles = product.astype(jnp.float32) * (2.0 * math.pi / length)
    norming = 1.0 / math.sqrt(length)
    cosine_table = jnp.cos(angles) * norming
    sine_table = jnp.sin(angles) * norming
    forward = (cosine_table, -sine_table - cosine_table, cosine_table - sine_table)
    inverse = (cosine_table, sine_table - cosine_table, cosine_table + sine_table)
    return (forward, inverse)


def complex_product(real_part, imag_part, matrices, pattern):
    first_term = jnp.einsum(
        pattern, real_part + imag_part, matrices[0], precision=lax.Precision.HIGHEST
    )
    second_term = jnp.einsum(pattern, real_part, matrices[1], precision=lax.Precision.HIGHEST)
    third_term = jnp.einsum(pattern, imag_part, matrices[2], precision=lax.Precision.HIGHEST)
    return (first_term - third_term, first_term + second_term)


def transform(real_part, imag_part, matrices):
    rows_real, rows_imag = complex_product(real_part, imag_part, matrices, "bjk,kw->bjw")
    return complex_product(rows_real, rows_imag, matrices, "bkw,jk->bjw")


def window_terms(win_real, win_imag, measured, probe_real, probe_imag, forward, inverse):
    psi_real = probe_real * win_real - probe_imag * win_imag
    psi_imag = probe_real * win_imag + probe_imag * win_real
    hat_real, hat_imag = transform(psi_real, psi_imag, forward)
    ratio_term = measured / jnp.sqrt(hat_real * hat_real + hat_imag * hat_imag + smooth_floor) - 1.0
    return transform(hat_real * ratio_term, hat_imag * ratio_term, inverse)


def add_window(grid_now, terms, first_row, first_col):
    zero_index = jnp.zeros((), jnp.int32)
    present = lax.dynamic_slice(grid_now, (zero_index, first_row, first_col), terms.shape)
    return lax.dynamic_update_slice(grid_now, present + terms, (zero_index, first_row, first_col))


def shards(object_field, probe_field, amplitudes, offsets, counts):
    tile_rows = object_field.shape[1]
    tile_cols = object_field.shape[2]
    window = probe_field.shape[1]
    slot_count = amplitudes.shape[0]
    margin = HALO
    forward, inverse = make_tables(window)
    count_here = counts[0, 0]
    current = object_field
    probe_now = probe_field
    for outer_step in range(OUTER):
        probe_real = probe_now[0]
        probe_imag = probe_now[1]
        probe_mean = jnp.sum(probe_now * probe_now) / (window * window)
        lower_rows = shifted(current[:, :margin, :], "row", -1)
        taller = jnp.concatenate([current, lower_rows], axis=1)
        right_cols = shifted(taller[:, :, :margin], "col", -1)
        extended = jnp.concatenate([taller, right_cols], axis=2)
        grad_ext = jnp.zeros_like(extended)
        zero_index = jnp.zeros((), jnp.int32)
        window_list = [
            lax.dynamic_slice(
                extended,
                (zero_index, offsets[0, 0, slot_index, 0], offsets[0, 0, slot_index, 1]),
                (2, window, window),
            )
            for slot_index in range(slot_count)
        ]
        stacked = jnp.stack(window_list, axis=1)
        win_real = stacked[0]
        win_imag = stacked[1]
        diff_real, diff_imag = window_terms(
            win_real, win_imag, amplitudes, probe_real, probe_imag, forward, inverse
        )
        live_mask = (jnp.arange(slot_count, dtype=jnp.int32) < count_here).astype(jnp.float32)[
            :, None, None
        ]
        diff_real = diff_real * live_mask
        diff_imag = diff_imag * live_mask
        object_real = probe_real * diff_real + probe_imag * diff_imag
        object_imag = probe_real * diff_imag - probe_imag * diff_real
        probe_grad = jnp.stack(
            [
                jnp.sum(win_real * diff_real + win_imag * diff_imag, axis=0),
                jnp.sum(win_real * diff_imag - win_imag * diff_real, axis=0),
            ]
        )
        power_sum = jnp.sum(live_mask * (win_real * win_real + win_imag * win_imag))
        for slot_index in range(slot_count):
            terms = jnp.stack([object_real[slot_index], object_imag[slot_index]])
            grad_ext = add_window(
                grad_ext, terms, offsets[0, 0, slot_index, 0], offsets[0, 0, slot_index, 1]
            )
        rim_right = shifted(grad_ext[:, :, tile_cols:], "col", 1)
        narrowed = grad_ext[:, :, :tile_cols]
        narrowed = jnp.concatenate(
            [narrowed[:, :, :margin] + rim_right, narrowed[:, :, margin:]], axis=2
        )
        rim_lower = shifted(narrowed[:, tile_rows:, :], "row", 1)
        tile_grad = jnp.concatenate(
            [narrowed[:, :margin, :] + rim_lower, narrowed[:, margin:tile_rows, :]], axis=1
        )
        current = current + object_step * tile_grad / (probe_mean + tiny_value)
        power_old = jnp.sum(probe_now * probe_now)
        summed_grad, summed_power = lax.psum((probe_grad, power_sum), ("row", "col"))
        moved_probe = probe_now + summed_grad / (summed_power / (window * window) + tiny_value)
        power_new = jnp.sum(moved_probe * moved_probe)
        probe_now = moved_probe * jnp.sqrt(power_old / (power_new + tiny_value))
    return (current, probe_now)


def solution(mesh):
    return jax.shard_map(
        shards,
        mesh=mesh,
        in_specs=(
            P(None, "row", "col"),
            P(),
            P("row", "col", None),
            P("row", "col", None, None),
            P("row", "col"),
        ),
        out_specs=(P(None, "row", "col"), P()),
        check_vma=False,
    )
```

profile of v0, /device:TPU:21, one launch (start us, length us, event | category | flops | bytes accessed | tf_op | source)
XLA Modules:
  0.0 694.5 jit_solution(13178830681612049637)
XLA Ops:
  8.2 10.7 %collective-permute-start = (f32[2,128,256]{2,1,0:T(8,128)S(1)}, f32[2,128,256]{2,1,0:T(8,128)S(1)}, u32[]{:S(2)}, u32[]{:S(2)}) collective-permute-start(f32[2,128,256]{2,1,0:T(8,128)S(1)} %slice.127), channel_id=1, source_target_pairs={{8,0},{16,8},{24,16},{32,24},{40,32},{48,40},{56,48},{64,56},{72,6... | collective-permute-start | bytes 786440 | tf_op jit(solution)/shard_map/ppermute | solution.py:17
  20.0 3.9 collective-permute-done
  23.9 3.4 collective-permute-start.1
  47.3 2.0 fusion.42
  49.3 1.8 convolution_add_fusion.5
  51.1 1.8 convolution_subtract_fusion.5
  54.5 1.7 fusion.9
  56.3 2.4 add_reduce_fusion.1
  59.6 7.6 %dynamic_update_slice.12 = f32[2,384,384]{2,1,0:T(8,128)S(1)} dynamic-update-slice(f32[2,384,384]{2,1,0:T(8,128)S(1)} %broadcast.28.clone, f32[2,256,256]{2,1,0:T(8,128)S(1)} %pad_maximum_fusion.3, s32[]{:T(128)} %constant.29.clone.1, s32[]{:T(128)S(6)} %select_n.82, s32[]{:T(128)S(6)} %select_n.83) | dynamic-update-slice | bytes 1048580 | tf_op jit(solution)/shard_map/dynamic_update_slice | solution.py:57
  68.4 7.0 %dynamic_update_slice.13 = f32[2,384,384]{2,1,0:T(8,128)S(1)} dynamic-update-slice(f32[2,384,384]{2,1,0:T(8,128)S(1)} %dynamic_update_slice.12, f32[2,256,256]{2,1,0:T(8,128)S(1)} %maximum_add_fusion, s32[]{:T(128)} %constant.29.clone.1, s32[]{:T(128)S(6)} %select_n.84, s32[]{:T(128)S(6)} %select_n.85) | dynamic-update-slice | bytes 1048580 | tf_op jit(solution)/shard_map/dynamic_update_slice | solution.py:57
  75.4 2.8 collective-permute-start.2
  79.1 3.8 collective-permute-done.2
  84.0 1.9 collective-permute-start.3
  86.0 101.0 %psum.29 = f32[]{:T(128)} all-reduce(f32[]{:T(128)} %get-tuple-element.7), channel_id=1, replica_groups=mesh['row'=64,'col'=8] {'row','col'}, use_global_device_ids=true, to_apply=%region_5.6 | all-reduce | flops 1 | bytes 8 | tf_op jit(solution)/shard_map/psum | solution.py:124
  187.6 165.8 %all-reduce.3.cloned.1.call-done = f32[2,256,256]{2,1,0:T(8,128)} async-done(((f32[2,256,256]{2,1,0:T(8,128)}), f32[2,256,256]{2,1,0:T(8,128)}) %all-reduce.3.cloned.1.call-update) | async-done | bytes 524304 | tf_op jit(solution)/shard_map/psum | solution.py:124
  353.4 1.8 multiply_reduce_fusion.3
  356.0 2.1 collective-permute-start.4
  359.4 6.7 collective-permute-done.4
  366.1 2.5 collective-permute-start.5
  368.8 6.5 collective-permute-done.5
  385.9 1.9 fusion.32
  387.8 1.8 convolution_add_fusion.1
  389.6 1.8 convolution_subtract_fusion.1
  394.7 2.4 add_reduce_fusion
  398.2 7.6 %dynamic_update_slice.14 = f32[2,384,384]{2,1,0:T(8,128)S(1)} dynamic-update-slice(f32[2,384,384]{2,1,0:T(8,128)S(1)} %broadcast.28, f32[2,256,256]{2,1,0:T(8,128)S(1)} %pad_maximum_fusion.5, s32[]{:T(128)} %constant.29.clone.1, s32[]{:T(128)S(6)} %select_n.82, s32[]{:T(128)S(6)} %select_n.83) | dynamic-update-slice | bytes 1048580 | tf_op jit(solution)/shard_map/dynamic_update_slice | solution.py:57
  406.0 7.0 %dynamic_update_slice.15 = f32[2,384,384]{2,1,0:T(8,128)S(1)} dynamic-update-slice(f32[2,384,384]{2,1,0:T(8,128)S(1)} %dynamic_update_slice.14, f32[2,256,256]{2,1,0:T(8,128)S(1)} %maximum_add_fusion.1, s32[]{:T(128)} %constant.29.clone.1, s32[]{:T(128)S(6)} %select_n.84, s32[]{:T(128)S(6)} %select_n.85) | dynamic-update-slice | bytes 1048580 | tf_op jit(solution)/shard_map/dynamic_update_slice | solution.py:57
  413.1 1.9 collective-permute-start.6
  415.0 98.3 %psum.31 = f32[]{:T(128)} all-reduce(f32[]{:T(128)} %get-tuple-element.6), channel_id=1, replica_groups=mesh['row'=64,'col'=8] {'row','col'}, use_global_device_ids=true, to_apply=%region_12.13 | all-reduce | flops 1 | bytes 8 | tf_op jit(solution)/shard_map/psum | solution.py:124
  514.0 155.3 %all-reduce.5.cloned.1.call-done = f32[2,256,256]{2,1,0:T(8,128)} async-done(((f32[2,256,256]{2,1,0:T(8,128)}), f32[2,256,256]{2,1,0:T(8,128)}) %all-reduce.5.cloned.1.call-update) | async-done | bytes 524304 | tf_op jit(solution)/shard_map/psum | solution.py:124
  669.3 1.8 multiply_reduce_fusion
  674.3 1.9 collective-permute-start.7
  677.1 9.3 %collective-permute-done.7 = f32[2,128,256]{2,1,0:T(8,128)S(1)} collective-permute-done((f32[2,128,256]{2,1,0:T(8,128)S(1)}, f32[2,128,256]{2,1,0:T(8,128)S(1)}, u32[]{:S(2)}, u32[]{:S(2)}) %collective-permute-start.7) | collective-permute-done | bytes 262176 | tf_op jit(solution)/shard_map/ppermute | solution.py:17
  (72 shorter events, 37.8 us)
Async XLA Ops:
  7.2 346.2 %all-reduce.3.cloned.1.call-start = ((), (), s32[]{:S(2)}) async-start(), calls=%async_computation | async-start | bytes 1048576 | tf_op jit(solution)/shard_map/psum | solution.py:124
  8.2 19.2 %copy-start.5 = (s32[1,1,2,2]{3,2,1,0:T(2,128)S(1)}, s32[1,1,2,2]{3,2,1,0:T(2,128)}, u32[]{:S(2)}) copy-start(s32[1,1,2,2]{3,2,1,0:T(2,128)} %param.8) | copy-start | bytes 52
  8.2 28.2 %copy-start.1 = (f32[2,256,256]{2,1,0:T(8,128)S(1)}, f32[2,256,256]{2,1,0:T(8,128)}, u32[]{:S(2)}) copy-start(f32[2,256,256]{2,1,0:T(8,128)} %param.6) | copy-start | bytes 1572868
  8.2 15.7 %collective-permute-start = (f32[2,128,256]{2,1,0:T(8,128)S(1)}, f32[2,128,256]{2,1,0:T(8,128)S(1)}, u32[]{:S(2)}, u32[]{:S(2)}) collective-permute-start(f32[2,128,256]{2,1,0:T(8,128)S(1)} %slice.127), channel_id=1, source_target_pairs={{8,0},{16,8},{24,16},{32,24},{40,32},{48,40},{56,48},{64,56},{72,6... | collective-permute-start | bytes 786440 | tf_op jit(solution)/shard_map/ppermute | solution.py:17
  23.9 12.5 %collective-permute-start.1 = (f32[2,384,128]{2,1,0:T(8,128)S(1)}, f32[2,384,128]{2,1,0:T(8,128)S(1)}, u32[]{:S(2)}, u32[]{:S(2)}) collective-permute-start(f32[2,384,128]{2,1,0:T(8,128)S(1)} %slice.162), channel_id=1, source_target_pairs={{1,0},{2,1},{3,2},{4,3},{5,4},{6,5},{7,6},{9,8},{10,9},{11,10},{12... | collective-permute-start | bytes 1179656 | tf_op jit(solution)/shard_map/ppermute | solution.py:17
  45.5 1.7 copy-start
  75.4 7.5 %collective-permute-start.2 = (f32[2,384,128]{2,1,0:T(8,128)S(1)}, f32[2,384,128]{2,1,0:T(8,128)}, u32[]{:S(2)}, u32[]{:S(2)}) collective-permute-start(f32[2,384,128]{2,1,0:T(8,128)S(1)} %slice.170), channel_id=1, source_target_pairs={{0,1},{1,2},{2,3},{3,4},{4,5},{5,6},{6,7},{8,9},{9,10},{10,11},{11... | collective-permute-start | bytes 1179656 | tf_op jit(solution)/shard_map/ppermute | solution.py:17
  79.1 590.2 %all-reduce.5.cloned.1.call-start = ((), (), s32[]{:S(2)}) async-start(), calls=%async_computation.1 | async-start | bytes 1048576 | tf_op jit(solution)/shard_map/psum | solution.py:124
  84.0 271.8 %collective-permute-start.3 = (f32[2,128,256]{2,1,0:T(8,128)S(1)}, f32[2,128,256]{2,1,0:T(8,128)S(1)}, u32[]{:S(2)}, u32[]{:S(2)}) collective-permute-start(f32[2,128,256]{2,1,0:T(8,128)S(1)} %fusion.56), channel_id=1, source_target_pairs={{0,8},{8,16},{16,24},{24,32},{32,40},{40,48},{48,56},{56,64},{64,7... | collective-permute-start | bytes 786440 | tf_op jit(solution)/shard_map/ppermute | solution.py:17
  187.6 168.3 %copy-start.2 = (f32[2,256,256]{2,1,0:T(8,128)S(1)}, f32[2,256,256]{2,1,0:T(8,128)}, u32[]{:S(2)}) copy-start(f32[2,256,256]{2,1,0:T(8,128)} %param.5) | copy-start | bytes 1572868
  356.0 12.6 %copy-start.4 = (f32[2,256,256]{2,1,0:T(8,128)S(1)}, f32[2,256,256]{2,1,0:T(8,128)}, u32[]{:S(2)}) copy-start(f32[2,256,256]{2,1,0:T(8,128)} %all-reduce.3.cloned.1.call-done) | copy-start | bytes 1572868
  356.0 10.1 %collective-permute-start.4 = (f32[2,128,256]{2,1,0:T(8,128)S(1)}, f32[2,128,256]{2,1,0:T(8,128)S(1)}, u32[]{:S(2)}, u32[]{:S(2)}) collective-permute-start(f32[2,128,256]{2,1,0:T(8,128)S(1)} %slice.177), channel_id=1, source_target_pairs={{8,0},{16,8},{24,16},{32,24},{40,32},{48,40},{56,48},{64,56},{72,6... | collective-permute-start | bytes 786440 | tf_op jit(solution)/shard_map/ppermute | solution.py:17
  366.1 9.1 %collective-permute-start.5 = (f32[2,384,128]{2,1,0:T(8,128)S(1)}, f32[2,384,128]{2,1,0:T(8,128)S(1)}, u32[]{:S(2)}, u32[]{:S(2)}) collective-permute-start(f32[2,384,128]{2,1,0:T(8,128)S(1)} %pad_maximum_fusion.7), channel_id=1, source_target_pairs={{1,0},{2,1},{3,2},{4,3},{5,4},{6,5},{7,6},{9,8},{10,9},{11,10},{12... | collective-permute-start | bytes 1179656 | tf_op jit(solution)/shard_map/ppermute | solution.py:17
  413.1 260.0 %collective-permute-start.6 = (f32[2,384,128]{2,1,0:T(8,128)S(1)}, f32[2,384,128]{2,1,0:T(8,128)}, u32[]{:S(2)}, u32[]{:S(2)}) collective-permute-start(f32[2,384,128]{2,1,0:T(8,128)S(1)} %slice.186), channel_id=1, source_target_pairs={{0,1},{1,2},{2,3},{3,4},{4,5},{5,6},{6,7},{8,9},{9,10},{10,11},{11... | collective-permute-start | bytes 1179656 | tf_op jit(solution)/shard_map/ppermute | solution.py:17
  673.1 3.1 copy-start.3
  674.3 12.1 %collective-permute-start.7 = (f32[2,128,256]{2,1,0:T(8,128)S(1)}, f32[2,128,256]{2,1,0:T(8,128)S(1)}, u32[]{:S(2)}, u32[]{:S(2)}) collective-permute-start(f32[2,128,256]{2,1,0:T(8,128)S(1)} %fusion.53), channel_id=1, source_target_pairs={{0,8},{8,16},{16,24},{24,32},{32,40},{40,48},{48,56},{56,64},{64,7... | collective-permute-start | bytes 786440 | tf_op jit(solution)/shard_map/ppermute | solution.py:17
Sparse Core Ops, SparseCore 0:
  79.2 274.1 all-reduce.2
  398.1 271.1 all-reduce.4
where the time goes:
time: 704 us; the launch traced here: 694 us
  waiting for transfers between devices  351 us (50%)
  blocking collectives  199 us (28%)
  matrix products  42.7 us (6%)
  local copies, waits for them, and re-layouts  33.5 us (5%)
  between operations  28.6 us (4%)
  starting transfers between devices  27.3 us (4%)
  other arithmetic  11.8 us (2%)
    psum x2, waiting for transfers between devices, shards(): lax.psum((probe_grad, power_sum), ('row', 'col'))  321 us
    psum x2, blocking collectives, shards(): lax.psum((probe_grad, power_sum), ('row', 'col'))  199 us
    ppermute x8, waiting for transfers between devices, shifted(): return lax.ppermute(value, axis, pairs)  30.1 us
    dynamic_update_slice x4, local copies, waits for them, and re-layouts, add_window(): lax.dynamic_update_slice(grid_now, present + terms, (zero_index, first_ro...  29.2 us
    ppermute x8, starting transfers between devices, shifted(): return lax.ppermute(value, axis, pairs)  27.2 us
    dot_general x8, matrix products, complex_product(): jnp.einsum(pattern, real_part, matrices[1], precision=lax.Precision.HIGHEST)  15.1 us
  transfers between devices with their start and end apart: 10, of which 7 were waited for; matrix products, arithmetic and copies ran while one was open for 3% of the time, Pallas kernels for 0%

commit v1 on v0

--- a/solution.py
+++ b/solution.py
@@ -121,7 +121,7 @@
         )
         current = current + object_step * tile_grad / (probe_mean + tiny_value)
         power_old = jnp.sum(probe_now * probe_now)
-        summed_grad, summed_power = lax.psum((probe_grad, power_sum), ("row", "col"))
+        summed_grad, summed_power = lax.psum(lax.psum((probe_grad, power_sum), "col"), "row")
         moved_probe = probe_now + summed_grad / (summed_power / (window * window) + tiny_value)
         power_new = jnp.sum(moved_probe * moved_probe)
         probe_now = moved_probe * jnp.sqrt(power_old / (power_new + tiny_value))

time: 704 us -> 624 us (0.89)
  the two profiles are of different devices: /device:TPU:21 before, /device:TPU:32 now
where the time goes in v1:
time: 624 us; the launch traced here: 614 us
  blocking collectives  312 us (50%)
  waiting for transfers between devices  153 us (25%)
  matrix products  43 us (7%)
  local copies, waits for them, and re-layouts  34 us (5%)
  starting transfers between devices  32.2 us (5%)
  between operations  28.4 us (5%)
  other arithmetic  11.7 us (2%)
    psum x2, blocking collectives, shards(): lax.psum(lax.psum((probe_grad, power_sum), 'col'), 'row')  284 us
    psum x2, waiting for transfers between devices, shards(): lax.psum((probe_grad, power_sum), 'col')  142 us
    ppermute x8, starting transfers between devices, shifted(): return lax.ppermute(value, axis, pairs)  32 us
    dynamic_update_slice x4, local copies, waits for them, and re-layouts, add_window(): lax.dynamic_update_slice(grid_now, present + terms, (zero_index, first_ro...  29.7 us
    psum x2, blocking collectives, shards(): lax.psum((probe_grad, power_sum), 'col')  27.8 us
    dot_general x8, matrix products, complex_product(): jnp.einsum(pattern, real_part, matrices[1], precision=lax.Precision.HIGHEST)  15.4 us
    dot_general x8, matrix products, complex_product(): jnp.einsum(pattern, real_part + imag_part, matrices[0], precision=lax.Pre...  13.8 us
    dot_general x8, matrix products, complex_product(): jnp.einsum(pattern, imag_part, matrices[2], precision=lax.Precision.HIGHEST)  13.8 us
  transfers between devices with their start and end apart: 12, of which 5 were waited for; matrix products, arithmetic and copies ran while one was open for 1% of the time, Pallas kernels for 0%

profile of v1, /device:TPU:32, one launch (start us, length us, event | category | flops | bytes accessed | tf_op | source)
XLA Modules:
  0.0 614.2 jit_solution(5505567327364875622)
XLA Ops:
  8.2 11.0 %collective-permute-start = (f32[2,128,256]{2,1,0:T(8,128)S(1)}, f32[2,128,256]{2,1,0:T(8,128)S(1)}, u32[]{:S(2)}, u32[]{:S(2)}) collective-permute-start(f32[2,128,256]{2,1,0:T(8,128)S(1)} %slice.127), channel_id=1, source_target_pairs={{8,0},{16,8},{24,16},{32,24},{40,32},{48,40},{56,48},{64,56},{72,6... | collective-permute-start | bytes 786440 | tf_op jit(solution)/shard_map/ppermute | solution.py:17
  20.3 4.5 collective-permute-done
  46.0 2.0 fusion.42
  48.1 1.8 convolution_add_fusion.5
  49.8 1.8 convolution_subtract_fusion.5
  53.2 1.7 fusion.9
  55.0 2.4 add_reduce_fusion.1
  58.3 7.4 %dynamic_update_slice.12 = f32[2,384,384]{2,1,0:T(8,128)S(1)} dynamic-update-slice(f32[2,384,384]{2,1,0:T(8,128)S(1)} %broadcast.28.clone, f32[2,256,256]{2,1,0:T(8,128)S(1)} %pad_maximum_fusion.3, s32[]{:T(128)} %constant.29.clone.1, s32[]{:T(128)S(6)} %select_n.82, s32[]{:T(128)S(6)} %select_n.83) | dynamic-update-slice | bytes 1048580 | tf_op jit(solution)/shard_map/dynamic_update_slice | solution.py:57
  66.9 7.4 %dynamic_update_slice.13 = f32[2,384,384]{2,1,0:T(8,128)S(1)} dynamic-update-slice(f32[2,384,384]{2,1,0:T(8,128)S(1)} %dynamic_update_slice.12, f32[2,256,256]{2,1,0:T(8,128)S(1)} %maximum_add_fusion, s32[]{:T(128)} %constant.29.clone.1, s32[]{:T(128)S(6)} %select_n.84, s32[]{:T(128)S(6)} %select_n.85) | dynamic-update-slice | bytes 1048580 | tf_op jit(solution)/shard_map/dynamic_update_slice | solution.py:57
  74.3 3.6 collective-permute-start.2
  78.9 71.8 %all-reduce.5.cloned.1.call-done = f32[2,256,256]{2,1,0:T(8,128)} async-done(((f32[2,256,256]{2,1,0:T(8,128)}), f32[2,256,256]{2,1,0:T(8,128)}) %all-reduce.5.cloned.1.call-update) | async-done | bytes 524304 | tf_op jit(solution)/shard_map/psum | solution.py:124
  151.8 3.6 collective-permute-start.3
  155.4 13.9 %psum.58 = f32[]{:T(128)} all-reduce(f32[]{:T(128)} %get-tuple-element.7), channel_id=1, replica_groups=mesh['row'=64,'col'=8] {'col'}, use_global_device_ids=true, to_apply=%region_6.7 | all-reduce | flops 1 | bytes 8 | tf_op jit(solution)/shard_map/psum | solution.py:124
  169.3 142.1 %psum.59 = f32[]{:T(128)} all-reduce(f32[]{:T(128)} %psum.58), channel_id=1, replica_groups=mesh['row'=64,'col'=8] {'row'}, use_global_device_ids=true, to_apply=%region_7.8 | all-reduce | flops 1 | bytes 8 | tf_op jit(solution)/shard_map/psum | solution.py:124
  312.1 1.8 multiply_reduce_fusion.3
  314.7 2.1 collective-permute-start.4
  318.2 4.9 collective-permute-done.4
  324.8 2.0 collective-permute-done.5
  334.0 1.7 fusion.4
  337.4 1.9 fusion.32
  339.3 1.7 convolution_add_fusion.1
  341.1 1.8 convolution_subtract_fusion.1
  344.5 1.7 fusion.3
  346.3 2.7 add_reduce_fusion
  349.2 7.4 %dynamic_update_slice.14 = f32[2,384,384]{2,1,0:T(8,128)S(1)} dynamic-update-slice(f32[2,384,384]{2,1,0:T(8,128)S(1)} %broadcast.28, f32[2,256,256]{2,1,0:T(8,128)S(1)} %pad_maximum_fusion.5, s32[]{:T(128)} %constant.29.clone.1, s32[]{:T(128)S(6)} %select_n.82, s32[]{:T(128)S(6)} %select_n.83) | dynamic-update-slice | bytes 1048580 | tf_op jit(solution)/shard_map/dynamic_update_slice | solution.py:57
  356.8 7.4 %dynamic_update_slice.15 = f32[2,384,384]{2,1,0:T(8,128)S(1)} dynamic-update-slice(f32[2,384,384]{2,1,0:T(8,128)S(1)} %dynamic_update_slice.14, f32[2,256,256]{2,1,0:T(8,128)S(1)} %maximum_add_fusion.1, s32[]{:T(128)} %constant.29.clone.1, s32[]{:T(128)S(6)} %select_n.84, s32[]{:T(128)S(6)} %select_n.85) | dynamic-update-slice | bytes 1048580 | tf_op jit(solution)/shard_map/dynamic_update_slice | solution.py:57
  364.3 5.4 collective-permute-start.6
  370.6 69.7 %all-reduce.9.cloned.1.call-done = f32[2,256,256]{2,1,0:T(8,128)} async-done(((f32[2,256,256]{2,1,0:T(8,128)}), f32[2,256,256]{2,1,0:T(8,128)}) %all-reduce.9.cloned.1.call-update) | async-done | bytes 524304 | tf_op jit(solution)/shard_map/psum | solution.py:124
  441.5 3.6 collective-permute-start.7
  445.0 13.9 %psum.62 = f32[]{:T(128)} all-reduce(f32[]{:T(128)} %get-tuple-element.6), channel_id=1, replica_groups=mesh['row'=64,'col'=8] {'col'}, use_global_device_ids=true, to_apply=%region_15.16 | all-reduce | flops 1 | bytes 8 | tf_op jit(solution)/shard_map/psum | solution.py:124
  459.0 142.0 %psum.63 = f32[]{:T(128)} all-reduce(f32[]{:T(128)} %psum.62), channel_id=1, replica_groups=mesh['row'=64,'col'=8] {'row'}, use_global_device_ids=true, to_apply=%region_16.17 | all-reduce | flops 1 | bytes 8 | tf_op jit(solution)/shard_map/psum | solution.py:124
  601.7 1.8 multiply_reduce_fusion
  (82 shorter events, 37.2 us)
Async XLA Ops:
  7.2 143.5 %all-reduce.5.cloned.1.call-start = ((), (), s32[]{:S(2)}) async-start(), calls=%async_computation | async-start | bytes 1048576 | tf_op jit(solution)/shard_map/psum | solution.py:124
  8.2 17.9 %copy-start.6 = (s32[1,1,2,2]{3,2,1,0:T(2,128)S(1)}, s32[1,1,2,2]{3,2,1,0:T(2,128)}, u32[]{:S(2)}) copy-start(s32[1,1,2,2]{3,2,1,0:T(2,128)} %param.8) | copy-start | bytes 52
  8.2 26.9 %copy-start.1 = (f32[2,256,256]{2,1,0:T(8,128)S(1)}, f32[2,256,256]{2,1,0:T(8,128)}, u32[]{:S(2)}) copy-start(f32[2,256,256]{2,1,0:T(8,128)} %param.6) | copy-start | bytes 1572868
  8.2 16.5 %collective-permute-start = (f32[2,128,256]{2,1,0:T(8,128)S(1)}, f32[2,128,256]{2,1,0:T(8,128)S(1)}, u32[]{:S(2)}, u32[]{:S(2)}) collective-permute-start(f32[2,128,256]{2,1,0:T(8,128)S(1)} %slice.127), channel_id=1, source_target_pairs={{8,0},{16,8},{24,16},{32,24},{40,32},{48,40},{56,48},{64,56},{72,6... | collective-permute-start | bytes 786440 | tf_op jit(solution)/shard_map/ppermute | solution.py:17
  24.8 10.3 %collective-permute-start.1 = (f32[2,384,128]{2,1,0:T(8,128)S(1)}, f32[2,384,128]{2,1,0:T(8,128)S(1)}, u32[]{:S(2)}, u32[]{:S(2)}) collective-permute-start(f32[2,384,128]{2,1,0:T(8,128)S(1)} %slice.162), channel_id=1, source_target_pairs={{1,0},{2,1},{3,2},{4,3},{5,4},{6,5},{7,6},{9,8},{10,9},{11,10},{12... | collective-permute-start | bytes 1179656 | tf_op jit(solution)/shard_map/ppermute | solution.py:17
  44.3 1.7 copy-start
  74.3 76.4 %collective-permute-start.2 = (f32[2,384,128]{2,1,0:T(8,128)S(1)}, f32[2,384,128]{2,1,0:T(8,128)}, u32[]{:S(2)}, u32[]{:S(2)}) collective-permute-start(f32[2,384,128]{2,1,0:T(8,128)S(1)} %slice.170), channel_id=1, source_target_pairs={{0,1},{1,2},{2,3},{3,4},{4,5},{5,6},{6,7},{8,9},{9,10},{10,11},{11... | collective-permute-start | bytes 1179656 | tf_op jit(solution)/shard_map/ppermute | solution.py:17
  78.8 233.3 %all-reduce.7.cloned.1.call-start = ((), (), s32[]{:S(2)}) async-start(), calls=%async_computation.1 | async-start | bytes 1048576 | tf_op jit(solution)/shard_map/psum | solution.py:124
  150.7 289.7 %all-reduce.9.cloned.1.call-start = ((), (), s32[]{:S(2)}) async-start(), calls=%async_computation.2 | async-start | bytes 1048576 | tf_op jit(solution)/shard_map/psum | solution.py:124
  151.8 160.2 %collective-permute-start.3 = (f32[2,128,256]{2,1,0:T(8,128)S(1)}, f32[2,128,256]{2,1,0:T(8,128)S(1)}, u32[]{:S(2)}, u32[]{:S(2)}) collective-permute-start(f32[2,128,256]{2,1,0:T(8,128)S(1)} %fusion.56), channel_id=1, source_target_pairs={{0,8},{8,16},{16,24},{24,32},{32,40},{40,48},{48,56},{56,64},{64,7... | collective-permute-start | bytes 786440 | tf_op jit(solution)/shard_map/ppermute | solution.py:17
  312.0 2.6 copy-start.2
  314.7 9.9 %copy-start.3 = (f32[2,256,256]{2,1,0:T(8,128)S(1)}, f32[2,256,256]{2,1,0:T(8,128)}, u32[]{:S(2)}) copy-start(f32[2,256,256]{2,1,0:T(8,128)} %all-reduce.7.cloned.1.call-done) | copy-start | bytes 1572868
  314.7 8.4 %collective-permute-start.4 = (f32[2,128,256]{2,1,0:T(8,128)S(1)}, f32[2,128,256]{2,1,0:T(8,128)S(1)}, u32[]{:S(2)}, u32[]{:S(2)}) collective-permute-start(f32[2,128,256]{2,1,0:T(8,128)S(1)} %slice.177), channel_id=1, source_target_pairs={{8,0},{16,8},{24,16},{32,24},{40,32},{48,40},{56,48},{64,56},{72,6... | collective-permute-start | bytes 786440 | tf_op jit(solution)/shard_map/ppermute | solution.py:17
  323.1 3.6 collective-permute-start.5
  356.8 12.9 %copy-start.5 = (f32[256,256]{1,0:T(8,128)S(1)}, f32[256,256]{1,0:T(8,128)}, u32[]{:S(2)}) copy-start(f32[256,256]{1,0:T(8,128)} %get-tuple-element.3) | copy-start | bytes 786436
  364.3 76.1 %collective-permute-start.6 = (f32[2,384,128]{2,1,0:T(8,128)S(1)}, f32[2,384,128]{2,1,0:T(8,128)}, u32[]{:S(2)}, u32[]{:S(2)}) collective-permute-start(f32[2,384,128]{2,1,0:T(8,128)S(1)} %slice.186), channel_id=1, source_target_pairs={{0,1},{1,2},{2,3},{3,4},{4,5},{5,6},{6,7},{8,9},{9,10},{10,11},{11... | collective-permute-start | bytes 1179656 | tf_op jit(solution)/shard_map/ppermute | solution.py:17
  370.5 231.2 %all-reduce.11.cloned.1.call-start = ((), (), s32[]{:S(2)}) async-start(), calls=%async_computation.3 | async-start | bytes 1048576 | tf_op jit(solution)/shard_map/psum | solution.py:124
  441.5 160.2 %collective-permute-start.7 = (f32[2,128,256]{2,1,0:T(8,128)S(1)}, f32[2,128,256]{2,1,0:T(8,128)S(1)}, u32[]{:S(2)}, u32[]{:S(2)}) collective-permute-start(f32[2,128,256]{2,1,0:T(8,128)S(1)} %fusion.53), channel_id=1, source_target_pairs={{0,8},{8,16},{16,24},{24,32},{32,40},{40,48},{48,56},{56,64},{64,7... | collective-permute-start | bytes 786440 | tf_op jit(solution)/shard_map/ppermute | solution.py:17
  603.5 2.9 copy-start.4
Sparse Core Ops, SparseCore 0:
  78.9 71.6 all-reduce.4
  153.9 155.0 all-reduce.6
  370.7 69.6 all-reduce.8
  443.4 154.9 all-reduce.10
